TPU v7x, 32 devices: a whole 2x2x4 slice. The times are simulated.
32 devices in a mesh: fsdp: 4 (over z), replica: 2 (over x), ctx: 4 (over y, core).
Axes of the slice: x: 2, y: 2, z: 4, core: 2. Of those that a mesh axis runs over, the one named last changes fastest.
Arguments:
- hidden_in: bfloat16 [8, 1088, 2048], P(('fsdp', 'replica'), 'ctx'), may hold values from -6 to 6
- memory_rows: bfloat16 [8, 50, 2048], P(('fsdp', 'replica')), may hold values from -6 to 6
- seg_len: int32 [8], P(('fsdp', 'replica')), may hold values from 519 to 1038, as said below
- out_grad: bfloat16 [8, 1088, 2048], P(('fsdp', 'replica'), 'ctx'), may hold values from -6 to 6
- first_gain: bfloat16 [2048], P('fsdp'), may hold values from 0.5 to 1.5
- first_shift: bfloat16 [2048], P('fsdp'), may hold values from -1 to 1
- qkv_weight: bfloat16 [2048, 6144], P('fsdp'), may hold values from -0.125 to 0.125
- query_bias: bfloat16 [2048], P('fsdp'), may hold values from -4 to 4
- value_bias: bfloat16 [2048], P('fsdp'), may hold values from -2.5 to 2.5
- out_weight: bfloat16 [2048, 2048], P('fsdp'), may hold values from -2 to 2
- out_bias: bfloat16 [2048], P('fsdp'), may hold values from -1 to 1
- second_gain: bfloat16 [2048], P('fsdp'), may hold values from 0.5 to 1.5
- second_shift: bfloat16 [2048], P('fsdp'), may hold values from -1 to 1
- up_weight: bfloat16 [2048, 8192], P('fsdp'), may hold values from -0.125 to 0.125
- up_bias: bfloat16 [8192], P('fsdp'), may hold values from -1 to 1
- down_weight: bfloat16 [8192, 2048], P('fsdp'), may hold values from -0.0625 to 0.0625
- down_bias: bfloat16 [2048], P('fsdp'), may hold values from -1 to 1
Outputs:
- output: bfloat16 [8, 1088, 2048], P(('fsdp', 'replica'), 'ctx')
- input_grad: float32 [8, 1088, 2048], P(('fsdp', 'replica'), 'ctx')
- memory_grad: float32 [8, 50, 2048], P(('fsdp', 'replica'))
- first_gain_grad: float32 [2048], P('fsdp')
- first_shift_grad: float32 [2048], P('fsdp')
- qkv_weight_grad: float32 [2048, 6144], P('fsdp')
- query_bias_grad: float32 [2048], P('fsdp')
- value_bias_grad: float32 [2048], P('fsdp')
- out_weight_grad: float32 [2048, 2048], P('fsdp')
- out_bias_grad: float32 [2048], P('fsdp')
- second_gain_grad: float32 [2048], P('fsdp')
- second_shift_grad: float32 [2048], P('fsdp')
- up_weight_grad: float32 [2048, 8192], P('fsdp')
- up_bias_grad: float32 [8192], P('fsdp')
- down_weight_grad: float32 [8192, 2048], P('fsdp')
- down_bias_grad: float32 [2048], P('fsdp')
Inputs may be any that keep to these rules, and one draw needn't show every extreme that they name: Positions seg_len to 1037 of a segment are padding that no query uses as a key.
All inputs are finite; a program needn't handle non-finite values.
Results may differ from a plain program's by a relative error of at most 0.015.
Values may be sent and summed in bfloat16 or wider, within the bound.
No kernel may reach another device: no remote copies, remote signals or barrier semaphores. Data moves between devices by JAX's collectives and lax.ppermute only.
A program may use at most 512 MiB of HBM per device.

v0:
```python
import jax
import jax.numpy as jnp
from jax import lax
from jax.sharding import PartitionSpec as P

D = 2048
HEADS = 32
HEAD_DIM = 64
SUMM = 50
SEQ_LEN = 1088
SEG = 1038
epsilon = 1e-05
masked = -1e30


def smooth_unit(values):
    return jax.nn.gelu(values, approximate=False)


def layer_norm(inputs, weight, offset):
    average = jnp.mean(inputs, axis=-1, keepdims=True)
    centred = inputs - average
    spread = jnp.mean(centred * centred, axis=-1, keepdims=True)
    inverse = lax.rsqrt(spread + epsilon)
    normal = centred * inverse
    return (normal * weight + offset, normal, inverse)


def norm_back(upstream, normal, inverse, weight):
    scaled = upstream * weight
    centre_term = jnp.mean(scaled, axis=-1, keepdims=True)
    slope_term = jnp.mean(scaled * normal, axis=-1, keepdims=True)
    return (
        inverse * (scaled - centre_term - normal * slope_term),
        jnp.sum(upstream * normal, axis=0),
        jnp.sum(upstream, axis=0),
    )


def across(left, right):
    return lax.dot_general(
        left, right, (((0,), (0,)), ((), ())), preferred_element_type=jnp.float32
    )


def against(left, right):
    return lax.dot_general(
        left, right, (((1,), (1,)), ((), ())), preferred_element_type=jnp.float32
    )


def head_slice(array, block_index, block_width, head_group):
    piece = lax.dynamic_slice_in_dim(array, block_index * block_width, block_width, 2)
    return piece.reshape(piece.shape[0], piece.shape[1], head_group, block_width // head_group)


def shards(
    hidden_in,
    memory_rows,
    seg_len,
    out_grad,
    first_gain,
    first_shift,
    qkv_weight,
    query_bias,
    value_bias,
    out_weight,
    out_bias,
    second_gain,
    second_shift,
    up_weight,
    up_bias,
    down_weight,
    down_bias,
):
    gathered = (
        lax.all_gather(first_gain, "fsdp", axis=0, tiled=True),
        lax.all_gather(first_shift, "fsdp", axis=0, tiled=True),
        lax.all_gather(qkv_weight, "fsdp", axis=0, tiled=True),
        lax.all_gather(query_bias, "fsdp", axis=0, tiled=True),
        lax.all_gather(value_bias, "fsdp", axis=0, tiled=True),
        lax.all_gather(out_weight, "fsdp", axis=0, tiled=True),
        lax.all_gather(out_bias, "fsdp", axis=0, tiled=True),
        lax.all_gather(second_gain, "fsdp", axis=0, tiled=True),
        lax.all_gather(second_shift, "fsdp", axis=0, tiled=True),
        lax.all_gather(up_weight, "fsdp", axis=0, tiled=True),
        lax.all_gather(up_bias, "fsdp", axis=0, tiled=True),
        lax.all_gather(down_weight, "fsdp", axis=0, tiled=True),
        lax.all_gather(down_bias, "fsdp", axis=0, tiled=True),
    )
    gain_one = gathered[0].astype(jnp.float32)
    shift_one = gathered[1].astype(jnp.float32)
    bias_query = gathered[3].astype(jnp.float32)
    bias_value = gathered[4].astype(jnp.float32)
    bias_out = gathered[6].astype(jnp.float32)
    gain_two = gathered[7].astype(jnp.float32)
    shift_two = gathered[8].astype(jnp.float32)
    bias_up = gathered[10].astype(jnp.float32)
    bias_down = gathered[12].astype(jnp.float32)
    weight_qkv = gathered[2]
    weight_out = gathered[5]
    weight_up = gathered[9]
    weight_down = gathered[11]
    groups = hidden_in.shape[0]
    span_rows = hidden_in.shape[1]
    row_count = groups * span_rows
    mem_count = groups * SUMM
    key_count = SUMM + SEQ_LEN
    head_group = min(8, HEADS)
    group_count = HEADS // head_group
    block_width = head_group * HEAD_DIM
    tokens = hidden_in.reshape(row_count, D).astype(jnp.float32)
    normed, normal_one, inverse_one = layer_norm(tokens, gain_one, shift_one)
    normed_low = normed.astype(jnp.bfloat16)
    memory = memory_rows.reshape(mem_count, D).astype(jnp.float32)
    mem_normed, mem_normal, mem_inverse = layer_norm(memory, gain_one, shift_one)
    mem_low = mem_normed.astype(jnp.bfloat16)
    projected = jnp.dot(normed_low, weight_qkv, preferred_element_type=jnp.float32)
    mem_projected = jnp.dot(mem_low, weight_qkv[:, D:], preferred_element_type=jnp.float32)
    query = (
        ((projected[:, :D] + bias_query) * 0.125).astype(jnp.bfloat16).reshape(groups, span_rows, D)
    )
    keys_local = projected[:, D : 2 * D].astype(jnp.bfloat16).reshape(groups, span_rows, D)
    values_local = (
        (projected[:, 2 * D :] + bias_value).astype(jnp.bfloat16).reshape(groups, span_rows, D)
    )
    mem_keys = mem_projected[:, :D].astype(jnp.bfloat16).reshape(groups, SUMM, D)
    mem_values = (mem_projected[:, D:] + bias_value).astype(jnp.bfloat16).reshape(groups, SUMM, D)
    keys_seq, values_seq = (
        lax.all_gather(keys_local, "ctx", axis=1, tiled=True),
        lax.all_gather(values_local, "ctx", axis=1, tiled=True),
    )
    keys_all = jnp.concatenate([mem_keys, keys_seq], axis=1)
    values_all = jnp.concatenate([mem_values, values_seq], axis=1)
    positions = lax.axis_index("ctx") * span_rows + jnp.arange(span_rows, dtype=jnp.int32)
    key_places = jnp.arange(SEQ_LEN, dtype=jnp.int32)
    causal = key_places[None, :] <= positions[:, None]
    present = (key_places[None, :] < seg_len[:, None]) | (key_places[None, :] >= SEG)
    allowed = jnp.concatenate(
        [jnp.ones((groups, span_rows, SUMM), dtype=bool), causal[None] & present[:, None, :]],
        axis=2,
    )[:, None]

    def attend(block_index):
        query_block = head_slice(query, block_index, block_width, head_group)
        key_block = head_slice(keys_all, block_index, block_width, head_group)
        value_block = head_slice(values_all, block_index, block_width, head_group)
        scores = jnp.einsum(
            "gqhd,gkhd->ghqk", query_block, key_block, preferred_element_type=jnp.float32
        )
        scores = jnp.where(allowed, scores, masked)
        largest = jnp.max(scores, axis=-1, keepdims=True)
        expanded = jnp.exp(scores - largest)
        totals = jnp.sum(expanded, axis=-1, keepdims=True)
        weights_low = (expanded / totals).astype(jnp.bfloat16)
        mixed_rows = jnp.einsum(
            "ghqk,gkhd->gqhd", weights_low, value_block, preferred_element_type=jnp.float32
        )
        return (mixed_rows.reshape(groups, span_rows, block_width), largest + jnp.log(totals))

    mixed_blocks, log_totals = lax.map(attend, jnp.arange(group_count))
    attended = jnp.moveaxis(mixed_blocks, 0, 2).reshape(row_count, D).astype(jnp.bfloat16)
    branch = jnp.dot(attended, weight_out, preferred_element_type=jnp.float32) + bias_out
    middle = tokens + branch
    normed_two, normal_two, inverse_two = layer_norm(middle, gain_two, shift_two)
    normed_two_low = normed_two.astype(jnp.bfloat16)
    upper = jnp.dot(normed_two_low, weight_up, preferred_element_type=jnp.float32) + bias_up
    active_float, smooth_pull = jax.vjp(smooth_unit, upper)
    active = active_float.astype(jnp.bfloat16)
    output = (
        (middle + (jnp.dot(active, weight_down, preferred_element_type=jnp.float32) + bias_down))
        .astype(jnp.bfloat16)
        .reshape(groups, span_rows, D)
    )
    again = (
        lax.all_gather(qkv_weight, "fsdp", axis=0, tiled=True),
        lax.all_gather(out_weight, "fsdp", axis=0, tiled=True),
        lax.all_gather(up_weight, "fsdp", axis=0, tiled=True),
        lax.all_gather(down_weight, "fsdp", axis=0, tiled=True),
    )
    back_qkv = again[0]
    back_out = again[1]
    back_up = again[2]
    back_down = again[3]
    cotangent = out_grad.reshape(row_count, D)
    cot_float = cotangent.astype(jnp.float32)
    down_part = lax.psum_scatter(
        across(active, cotangent).astype(jnp.bfloat16), "fsdp", scatter_dimension=0, tiled=True
    ).astype(jnp.float32)
    hidden_grad = against(cotangent, back_down)
    upper_grad = smooth_pull(hidden_grad)[0].astype(jnp.bfloat16)
    up_part = lax.psum_scatter(
        across(normed_two_low, upper_grad).astype(jnp.bfloat16),
        "fsdp",
        scatter_dimension=0,
        tiled=True,
    ).astype(jnp.float32)
    normed_two_grad = against(upper_grad, back_up)
    middle_norm_grad, gain_two_grad, shift_two_grad = norm_back(
        normed_two_grad, normal_two, inverse_two, gain_two
    )
    middle_grad = cot_float + middle_norm_grad
    branch_grad = middle_grad.astype(jnp.bfloat16)
    out_weight_grad = across(attended, branch_grad)
    mixed_grad = against(branch_grad, back_out).astype(jnp.bfloat16).reshape(groups, span_rows, D)

    def attend_back(block_index):
        query_block = head_slice(query, block_index, block_width, head_group)
        key_block = head_slice(keys_all, block_index, block_width, head_group)
        value_block = head_slice(values_all, block_index, block_width, head_group)
        grad_block = head_slice(mixed_grad, block_index, block_width, head_group)
        scores = jnp.einsum(
            "gqhd,gkhd->ghqk", query_block, key_block, preferred_element_type=jnp.float32
        )
        scores = jnp.where(allowed, scores, masked)
        weights = jnp.exp(scores - log_totals[block_index])
        value_grad = jnp.einsum(
            "ghqk,gqhd->gkhd",
            weights.astype(jnp.bfloat16),
            grad_block,
            preferred_element_type=jnp.float32,
        )
        weight_grad = jnp.einsum(
            "gqhd,gkhd->ghqk", grad_block, value_block, preferred_element_type=jnp.float32
        )
        centre = jnp.sum(weights * weight_grad, axis=-1, keepdims=True)
        score_grad = (weights * (weight_grad - centre)).astype(jnp.bfloat16)
        query_grad = jnp.einsum(
            "ghqk,gkhd->gqhd", score_grad, key_block, preferred_element_type=jnp.float32
        )
        key_grad = jnp.einsum(
            "ghqk,gqhd->gkhd", score_grad, query_block, preferred_element_type=jnp.float32
        )
        return (
            query_grad.reshape(groups, span_rows, block_width),
            key_grad.reshape(groups, key_count, block_width),
            value_grad.reshape(groups, key_count, block_width),
        )

    query_blocks, key_blocks, value_blocks = lax.map(attend_back, jnp.arange(group_count))
    query_grad_all = jnp.moveaxis(query_blocks, 0, 2).reshape(groups, span_rows, D)
    key_grad_all = jnp.moveaxis(key_blocks, 0, 2).reshape(groups, key_count, D)
    value_grad_all = jnp.moveaxis(value_blocks, 0, 2).reshape(groups, key_count, D)
    key_sums, value_sums = (
        lax.psum_scatter(key_grad_all[:, SUMM:], "ctx", scatter_dimension=1, tiled=True),
        lax.psum_scatter(value_grad_all[:, SUMM:], "ctx", scatter_dimension=1, tiled=True),
    )
    mem_key_sums, mem_value_sums = lax.psum(
        (key_grad_all[:, :SUMM], value_grad_all[:, :SUMM]), "ctx"
    )
    qkv_grad = jnp.concatenate(
        [
            query_grad_all.astype(jnp.bfloat16) * 0.125,
            key_sums.astype(jnp.bfloat16),
            value_sums.astype(jnp.bfloat16),
        ],
        axis=2,
    ).reshape(row_count, 3 * D)
    mem_kv_grad = jnp.concatenate(
        [mem_key_sums.astype(jnp.bfloat16), mem_value_sums.astype(jnp.bfloat16)], axis=2
    ).reshape(mem_count, 2 * D)
    owner_flag = lax.axis_index("ctx") == 0
    first_owner = owner_flag.astype(jnp.float32)
    owned_mem_grad = jnp.where(owner_flag, mem_kv_grad, jnp.zeros_like(mem_kv_grad))
    mem_rows_grad = jnp.concatenate(
        [jnp.zeros((mem_count, D), jnp.bfloat16), owned_mem_grad], axis=1
    )
    qkv_weight_grad = across(
        jnp.concatenate([normed_low, mem_low], axis=0),
        jnp.concatenate([qkv_grad, mem_rows_grad], axis=0),
    )
    query_bias_grad = jnp.sum(qkv_grad[:, :D].astype(jnp.float32), axis=0)
    value_bias_grad = jnp.sum(qkv_grad[:, 2 * D :].astype(jnp.float32), axis=0) + jnp.sum(
        owned_mem_grad[:, D:].astype(jnp.float32), axis=0
    )
    out_bias_grad = jnp.sum(branch_grad.astype(jnp.float32), axis=0)
    up_bias_grad = jnp.sum(upper_grad.astype(jnp.float32), axis=0)
    down_bias_grad = jnp.sum(cot_float, axis=0)
    normed_grad = against(qkv_grad, back_qkv)
    token_norm_grad, gain_one_tok, shift_one_tok = norm_back(
        normed_grad, normal_one, inverse_one, gain_one
    )
    mem_normed_grad = against(mem_kv_grad, back_qkv[:, D:])
    memory_norm_grad, gain_one_mem, shift_one_mem = norm_back(
        mem_normed_grad, mem_normal, mem_inverse, gain_one
    )
    gain_one_grad = gain_one_tok + first_owner * gain_one_mem
    shift_one_grad = shift_one_tok + first_owner * shift_one_mem
    input_grad = (middle_grad + token_norm_grad).reshape(groups, span_rows, D)
    memory_grad = memory_norm_grad.reshape(groups, SUMM, D)
    shares = (
        lax.psum_scatter(
            gain_one_grad.astype(jnp.bfloat16), "fsdp", scatter_dimension=0, tiled=True
        ).astype(jnp.float32),
        lax.psum_scatter(
            shift_one_grad.astype(jnp.bfloat16), "fsdp", scatter_dimension=0, tiled=True
        ).astype(jnp.float32),
        lax.psum_scatter(
            qkv_weight_grad.astype(jnp.bfloat16), "fsdp", scatter_dimension=0, tiled=True
        ).astype(jnp.float32),
        lax.psum_scatter(
            query_bias_grad.astype(jnp.bfloat16), "fsdp", scatter_dimension=0, tiled=True
        ).astype(jnp.float32),
        lax.psum_scatter(
            value_bias_grad.astype(jnp.bfloat16), "fsdp", scatter_dimension=0, tiled=True
        ).astype(jnp.float32),
        lax.psum_scatter(
            out_weight_grad.astype(jnp.bfloat16), "fsdp", scatter_dimension=0, tiled=True
        ).astype(jnp.float32),
        lax.psum_scatter(
            out_bias_grad.astype(jnp.bfloat16), "fsdp", scatter_dimension=0, tiled=True
        ).astype(jnp.float32),
        lax.psum_scatter(
            gain_two_grad.astype(jnp.bfloat16), "fsdp", scatter_dimension=0, tiled=True
        ).astype(jnp.float32),
        lax.psum_scatter(
            shift_two_grad.astype(jnp.bfloat16), "fsdp", scatter_dimension=0, tiled=True
        ).astype(jnp.float32),
        lax.psum_scatter(
            up_bias_grad.astype(jnp.bfloat16), "fsdp", scatter_dimension=0, tiled=True
        ).astype(jnp.float32),
        lax.psum_scatter(
            down_bias_grad.astype(jnp.bfloat16), "fsdp", scatter_dimension=0, tiled=True
        ).astype(jnp.float32),
    )
    summed = lax.psum(
        (
            shares[0],
            shares[1],
            shares[2],
            shares[3],
            shares[4],
            shares[5],
            shares[6],
            shares[7],
            shares[8],
            shares[9],
            shares[10],
            up_part,
            down_part,
        ),
        ("replica", "ctx"),
    )
    return (
        output,
        input_grad,
        memory_grad,
        summed[0],
        summed[1],
        summed[2],
        summed[3],
        summed[4],
        summed[5],
        summed[6],
        summed[7],
        summed[8],
        summed[11],
        summed[9],
        summed[12],
        summed[10],
    )


def solution(mesh):
    return jax.shard_map(
        shards,
        mesh=mesh,
        in_specs=(
            P(("fsdp", "replica"), "ctx", None),
            P(("fsdp", "replica"), None, None),
            P(("fsdp", "replica")),
            P(("fsdp", "replica"), "ctx", None),
            P("fsdp"),
            P("fsdp"),
            P("fsdp", None),
            P("fsdp"),
            P("fsdp"),
            P("fsdp", None),
            P("fsdp"),
            P("fsdp"),
            P("fsdp"),
            P("fsdp", None),
            P("fsdp"),
            P("fsdp", None),
            P("fsdp"),
        ),
        out_specs=(
            P(("fsdp", "replica"), "ctx", None),
            P(("fsdp", "replica"), "ctx", None),
            P(("fsdp", "replica"), None, None),
            P("fsdp"),
            P("fsdp"),
            P("fsdp", None),
            P("fsdp"),
            P("fsdp"),
            P("fsdp", None),
            P("fsdp"),
            P("fsdp"),
            P("fsdp"),
            P("fsdp", None),
            P("fsdp"),
            P("fsdp", None),
            P("fsdp"),
        ),
        check_vma=False,
    )
```

profile of v0, /device:TPU:1, one launch (start us, length us, event | category | flops | bytes accessed | tf_op | source)
XLA Modules:
  0.0 7154.1 jit_solution(2888771679025506342)
XLA Ops:
  8.7 10.3 all-gather.3
  19.7 9.3 all-gather.2
  29.7 36.0 all-gather.5
  66.3 33.2 all-gather.4
  100.8 336.6 %all-gather.17.cloned.1.call-done = bf16[2048,6144]{1,0:T(8,128)(2,1)} async-done(((bf16[512,6144]{1,0:T(8,128)(2,1)}), bf16[2048,6144]{1,0:T(8,128)(2,1)}) %all-gather.17.cloned.1.call-update) | async-done | bytes 25165840 | tf_op jit(solution)/shard_map/all_gather | solution.py:79
  437.4 11.9 fusion.87
  458.9 9.7 all-gather.6
  469.3 10.2 all_gather.61
  479.6 9.7 all-gather.8
  489.3 9.3 all-gather.7
  503.1 7.4 fusion.7
  516.6 6.7 copy.54
  532.8 6.9 copy.56
  540.9 48.0 while.26
  589.0 88.8 %all-gather.19.cloned.1.call-done = bf16[2048,2048]{1,0:T(8,128)(2,1)} async-done(((bf16[512,2048]{1,0:T(8,128)(2,1)}), bf16[2048,2048]{1,0:T(8,128)(2,1)}) %all-gather.19.cloned.1.call-update) | async-done | bytes 8388624 | tf_op jit(solution)/shard_map/all_gather | solution.py:82
  677.7 6.6 fusion.82
  686.1 552.7 %all-gather.21.cloned.1.call-done = bf16[2048,8192]{1,0:T(8,128)(2,1)} async-done(((bf16[512,8192]{1,0:T(8,128)(2,1)}), bf16[2048,8192]{1,0:T(8,128)(2,1)}) %all-gather.21.cloned.1.call-update) | async-done | bytes 33554448 | tf_op jit(solution)/shard_map/all_gather | solution.py:86
  1238.8 34.7 multiply_convert_fusion.1
  1273.5 526.4 %all-gather.23.cloned.1.call-done = bf16[8192,2048]{1,0:T(8,128)(2,1)} async-done(((bf16[2048,2048]{1,0:T(8,128)(2,1)}), bf16[8192,2048]{1,0:T(8,128)(2,1)}) %all-gather.23.cloned.1.call-update) | async-done | bytes 33554448 | tf_op jit(solution)/shard_map/all_gather | solution.py:88
  1799.8 36.5 fusion.83
  1836.4 17.0 multiply_reduce_fusion.1
  1854.9 6.8 convolution_convert_fusion.3
  1862.0 6.9 fusion.32
  1870.2 188.6 %while.27 = (s32[]{:T(128)}, bf16[4,1,272,512]{2,3,1,0:T(8,128)(2,1)}, f32[4,1,1138,512]{2,3,1,0:T(8,128)}, f32[4,1,1138,512]{2,3,1,0:T(8,128)}, s32[4]{0:T(128)...) while((s32[]{:T(128)}, ...), condition=%wide.region_14.15_spmd, body=%wide.region_12.14_spmd.sunk | while | flops 1604632448 | bytes 115616344 | solution.py:240
  1884.6 8.4 multiply_reduce_fusion.8
  1893.0 10.1 multiply_convert_fusion.3
  1931.8 8.3 multiply_reduce_fusion.8
  1940.1 10.1 multiply_convert_fusion.3
  1978.8 8.4 multiply_reduce_fusion.8
  1987.2 10.1 multiply_convert_fusion.3
  2026.1 8.3 multiply_reduce_fusion.8
  2034.4 10.0 multiply_convert_fusion.3
  2060.4 10.1 slice.62
  2077.8 21.4 copy.74
  2099.3 21.4 copy.73
  2120.7 2492.1 %all-reduce.20 = (bf16[1,50,2048]{2,0,1:T(2,128)(2,1)S(1)}, bf16[1,50,2048]{2,0,1:T(2,128)(2,1)S(1)}, bf16[1,1088,2048]{2,0,1:T(2,128)(2,1)}, bf16[1,1088,2048]{2,0,1:T(2,128)(2,1)}) all-reduce(f32[1,50,2048]{2,0,1:T(1,128)S(1)} %copy.76, f32[1,50,2048]{2,0,1:T(1,128)S(1)} %copy.75, ...), channel_id=1, replica_groups=mesh['fsdp'=4,'replica'=2,'ctx'=4] {'ctx'}, use_global_device_ids=true, to_apply=%region_20.21 | all-reduce | flops 4661248 | bytes 27967488 | tf_op jit(solution)/shard_map/psum | solution.py:248
  4629.4 17.2 convolution_convert_fusion.2
  4648.3 24.3 convolution_convert_fusion.1
  4673.8 24.3 convolution_convert_fusion
  4698.8 11.8 all-gather.9
  4712.8 12.2 fusion.69
  4731.5 14.9 fusion.40
  4746.5 19.0 all-reduce.17
  4770.6 17.5 fusion.31
  4788.1 272.3 %reduce-scatter.9.cloned.1.call-done = bf16[512,6144]{1,0:T(8,128)(2,1)} async-done(((bf16[2048,6144]{1,0:T(8,128)(2,1)}), bf16[512,6144]{1,0:T(8,128)(2,1)}) %reduce-scatter.9.cloned.1.call-update) | async-done | bytes 6291472 | tf_op jit(solution)/shard_map/reduce_scatter | solution.py:298
  5060.4 556.3 %reduce-scatter.13.cloned.1.call-done = bf16[512,8192]{1,0:T(8,128)(2,1)} async-done(((bf16[2048,8192]{1,0:T(8,128)(2,1)}), bf16[512,8192]{1,0:T(8,128)(2,1)}) %reduce-scatter.13.cloned.1.call-update) | async-done | bytes 8388624
  5616.7 555.0 %reduce-scatter.15.cloned.1.call-done = bf16[2048,2048]{1,0:T(8,128)(2,1)} async-done(((bf16[8192,2048]{1,0:T(8,128)(2,1)}), bf16[2048,2048]{1,0:T(8,128)(2,1)}) %reduce-scatter.15.cloned.1.call-update) | async-done | bytes 8388624
  6171.8 975.3 %all-reduce.21 = (f32[512]{0:T(512)}, f32[512]{0:T(512)}, f32[512,6144]{1,0:T(8,128)}, f32[512]{0:T(512)}, f32[512]{0:T(512)}, /*index=5*/f32[512,2048]{1,0:T(8,...) all-reduce(f32[512]{0:T(512)S(1)} %dynamic-slice_convert_fusion.8, ...), channel_id=1, replica_groups=mesh['fsdp'=4,'replica'=2,'ctx'=4] {'replica','ctx'}, use_global_device_ids=true, to_apply=%region_26.27 | all-reduce | flops 12589056 | bytes 75546624 | tf_op jit(solution)/shard_map/psum | solution.py:326
  (332 shorter events, 229.7 us)
Async XLA Ops:
  7.2 92.4 %copy-start.2 = (bf16[1,272,2048]{2,1,0:T(8,128)(2,1)S(1)}, bf16[1,272,2048]{2,1,0:T(8,128)(2,1)}, u32[]{:S(2)}) copy-start(bf16[1,272,2048]{2,1,0:T(8,128)(2,1)} %param.21) | copy-start | bytes 3342340
  7.2 430.2 %all-gather.17.cloned.1.call-start = ((), (), s32[]{:S(2)}) async-start(), calls=%async_computation.4 | async-start | bytes 31457280 | tf_op jit(solution)/shard_map/all_gather | solution.py:79
  7.9 502.7 %all-gather.25.cloned.1.call-start = ((), (), s32[]{:S(2)}) async-start(), calls=%async_computation.10 | async-start | bytes 5570560 | tf_op jit(solution)/shard_map/all_gather | solution.py:131
  29.0 472.0 %copy-start.25 = (f32[4,1,512]{2,1,0:T(1,128)}, f32[4,1,512]{2,1,0:T(1,128)S(1)}, u32[]{:S(2)}) copy-start(f32[4,1,512]{2,1,0:T(1,128)S(1)} %convert_element_type.263) | copy-start | bytes 24580
  99.8 349.5 %copy-start.29 = (f32[272]{0:T(512)}, f32[272]{0:T(512)S(1)}, u32[]{:S(2)}) copy-start(f32[272]{0:T(512)S(1)} %broadcast_multiply_fusion.5) | copy-start | bytes 3268
  100.3 349.1 %copy-start.33 = (f32[272]{0:T(512)}, f32[272]{0:T(512)S(1)}, u32[]{:S(2)}) copy-start(f32[272]{0:T(512)S(1)} %add_rsqrt_fusion.1) | copy-start | bytes 3268
  100.8 348.6 %copy-start.18 = (bf16[272,2048]{1,0:T(8,128)(2,1)}, bf16[272,2048]{1,0:T(8,128)(2,1)S(1)}, u32[]{:S(2)}) copy-start(bf16[272,2048]{1,0:T(8,128)(2,1)S(1)} %fusion.34) | copy-start | bytes 3342340
  454.2 72.7 %all-gather.27.cloned.1.call-start = ((), (), s32[]{:S(2)}) async-start(), calls=%async_computation.11 | async-start | bytes 5570560 | tf_op jit(solution)/shard_map/all_gather | solution.py:130
  457.0 220.7 %all-gather.19.cloned.1.call-start = ((), (), s32[]{:S(2)}) async-start(), calls=%async_computation.5 | async-start | bytes 10485760 | tf_op jit(solution)/shard_map/all_gather | solution.py:82
  457.6 11.7 copy-start.43
  457.6 21.9 copy-start.49
  457.6 31.6 copy-start.50
  457.6 41.0 copy-start.53
  457.7 42.2 copy-start.17
  457.7 781.1 %all-gather.21.cloned.1.call-start = ((), (), s32[]{:S(2)}) async-start(), calls=%async_computation.6 | async-start | bytes 41943040 | tf_op jit(solution)/shard_map/all_gather | solution.py:86
  458.3 1341.6 %all-gather.23.cloned.1.call-start = ((), (), s32[]{:S(2)}) async-start(), calls=%async_computation.7 | async-start | bytes 41943040 | tf_op jit(solution)/shard_map/all_gather | solution.py:88
  458.8 4329.3 %reduce-scatter.11.cloned.1.call-start = ((), (), s32[]{:S(2)}) async-start(), calls=%async_computation.9 | async-start | bytes 10485760 | tf_op jit(solution)/shard_map/reduce_scatter | solution.py:307
  489.3 749.5 %copy-start.39 = (f32[4,1,512]{2,1,0:T(1,128)}, f32[4,1,512]{2,1,0:T(1,128)S(1)}, u32[]{:S(2)}) copy-start(f32[4,1,512]{2,1,0:T(1,128)S(1)} %convert_element_type.269) | copy-start | bytes 24580
  498.6 1354.8 %copy-start.27 = (f32[4,1,512]{2,1,0:T(1,128)}, f32[4,1,512]{2,1,0:T(1,128)S(1)}, u32[]{:S(2)}) copy-start(f32[4,1,512]{2,1,0:T(1,128)S(1)} %convert_element_type.268) | copy-start | bytes 24580
  500.0 10.5 copy-start.41
  500.3 10.2 copy-start.46
  589.0 95.4 %copy-start = (pred[1,1,272,1138]{3,2,1,0:T(8,128)(4,1)}, pred[1,1,272,1138]{3,2,1,0:T(8,128)(4,1)S(1)}, u32[]{:S(2)}) copy-start(pred[1,1,272,1138]{3,2,1,0:T(8,128)(4,1)S(1)} %get-tuple-element.553) | copy-start | bytes 928612
  589.0 95.4 %copy-start.7 = (bf16[1,272,2048]{1,2,0:T(8,128)(2,1)}, bf16[1,272,2048]{1,2,0:T(8,128)(2,1)S(1)}, u32[]{:S(2)}) copy-start(bf16[1,272,2048]{1,2,0:T(8,128)(2,1)S(1)} %get-tuple-element.562) | copy-start | bytes 3342340
  684.4 1169.1 %copy-start.31 = (f32[272]{0:T(512)}, f32[272]{0:T(512)S(1)}, u32[]{:S(2)}) copy-start(f32[272]{0:T(512)S(1)} %broadcast_multiply_fusion.4) | copy-start | bytes 3268
  686.1 1167.3 %copy-start.37 = (f32[272]{0:T(512)}, f32[272]{0:T(512)S(1)}, u32[]{:S(2)}) copy-start(f32[272]{0:T(512)S(1)} %add_rsqrt_fusion) | copy-start | bytes 3268
  1238.8 561.0 %copy-start.13 = (bf16[1,272,2048]{2,1,0:T(8,128)(2,1)S(1)}, bf16[1,272,2048]{2,1,0:T(8,128)(2,1)}, u32[]{:S(2)}) copy-start(bf16[1,272,2048]{2,1,0:T(8,128)(2,1)} %param.24) | copy-start | bytes 3342340
  1799.8 36.5 copy-start.5
  1836.4 17.1 copy-start.14
  1854.9 7.1 copy-start.9
  1861.8 8.4 copy-start.1
  1861.8 3198.6 %reduce-scatter.9.cloned.1.call-start = ((), (), s32[]{:S(2)}) async-start(), calls=%async_computation.8 | async-start | bytes 31457280 | tf_op jit(solution)/shard_map/reduce_scatter | solution.py:298
  2058.9 11.6 slice-start.2
  2060.3 10.1 slice-start.3
  2060.3 10.1 slice-start.4
  4617.4 8.2 copy-start.16
  4646.7 970.0 %reduce-scatter.13.cloned.1.call-start = ((), (), s32[]{:S(2)}) async-start(), calls=%async_computation.12 | async-start | bytes 41943040
  4672.6 1499.1 %reduce-scatter.15.cloned.1.call-start = ((), (), s32[]{:S(2)}) async-start(), calls=%async_computation.13 | async-start | bytes 41943040
  4698.1 12.7 copy-start.52
  4698.1 14.6 copy-start.26
  4698.1 14.6 copy-start.42
  4698.2 14.6 copy-start.47
  4712.8 18.7 copy-start.3
  4712.8 18.7 copy-start.30
  4712.8 18.7 copy-start.34
  4731.5 15.0 copy-start.35
  4731.5 15.0 copy-start.36
  4731.5 15.0 copy-start.44
  4731.5 15.0 copy-start.45
  (27 other events, 90.5 us)
Sparse Core Ops, SparseCore 0:
  9.6 427.7 all-gather.16
  454.3 34.3 all-gather.24
  490.8 35.9 all-gather.26
  528.2 149.4 all-gather.18
  679.1 559.6 all-gather.20
  1240.2 559.5 all-gather.22
  1861.9 142.2 reduce-scatter.10
  4646.8 413.5 reduce-scatter.8
  5062.9 553.7 reduce-scatter.12
  5619.0 552.7 reduce-scatter.14
where the time goes:
time: 7170 us; the launch traced here: 7150 us
  blocking collectives  3630 us (51%)
  waiting for transfers between devices  2890 us (40%)
  matrix products  356 us (5%)
  local copies, waits for them, and re-layouts  161 us (2%)
  other arithmetic  84.4 us (1%)
    psum x1, blocking collectives, shards(): lax.psum((key_grad_all[:, :SUMM], value_grad_all[:, :SUMM]), 'ctx')  2490 us
    unnamed x12, waiting for transfers between devices  1110 us
    psum x1, blocking collectives, shards(): lax.psum((shares[0], shares[1], shares[2], shares[3], shares[4], shares[5...  975 us
    all_gather x1, waiting for transfers between devices, shards(): lax.all_gather(up_weight, 'fsdp', axis=0, tiled=True)  553 us
    all_gather x1, waiting for transfers between devices, shards(): lax.all_gather(down_weight, 'fsdp', axis=0, tiled=True)  526 us
    all_gather x1, waiting for transfers between devices, shards(): lax.all_gather(qkv_weight, 'fsdp', axis=0, tiled=True)  337 us
    reduce_scatter x1, waiting for transfers between devices, shards(): lax.psum_scatter(qkv_weight_grad.astype(jnp.bfloat16), 'fsdp', scatter_di...  272 us
  transfers between devices with their start and end apart: 10, of which 8 were waited for; matrix products, arithmetic and copies ran while one was open for 7% of the time, Pallas kernels for 0%

commit v1 on v0

--- a/solution.py
+++ b/solution.py
@@ -11,6 +11,19 @@
 SEG = 1038
 epsilon = 1e-05
 masked = -1e30
+
+
+def ring_gather(x, axis, dim):
+    ways = lax.axis_size(axis)
+    up = [(d, (d + 1) % ways) for d in range(ways)]
+    down = [(d, (d - 1) % ways) for d in range(ways)]
+    earlier, later = ([x], [x])
+    for _ in range(ways // 2):
+        earlier.append(lax.ppermute(earlier[-1], axis, up))
+    for _ in range((ways - 1) // 2):
+        later.append(lax.ppermute(later[-1], axis, down))
+    line = jnp.concatenate([*earlier[::-1], *later[1:]], axis=dim)
+    return jnp.roll(line, (lax.axis_index(axis) - ways // 2) * x.shape[dim], axis=dim)
 
 
 def smooth_unit(values):
@@ -85,7 +98,7 @@
         lax.all_gather(second_shift, "fsdp", axis=0, tiled=True),
         lax.all_gather(up_weight, "fsdp", axis=0, tiled=True),
         lax.all_gather(up_bias, "fsdp", axis=0, tiled=True),
-        lax.all_gather(down_weight, "fsdp", axis=0, tiled=True),
+        ring_gather(down_weight, "fsdp", 0),
         lax.all_gather(down_bias, "fsdp", axis=0, tiled=True),
     )
     gain_one = gathered[0].astype(jnp.float32)

time: 7170 us -> 7710 us (1.075)
  blocking collectives: 3630 us -> 4110 us
  local copies, waits for them, and re-layouts: 161 us -> 241 us
    all_gather x1, blocking collectives: 11.8 us -> 495 us  [shards(): lax.all_gather(down_bias, 'fsdp', axis=0, tiled=True)]
    ppermute x0 -> x3, waiting for transfers between devices: none -> 364 us  [the longest x2 364 us: ring_gather(): earlier.append(lax.ppermute(earlier[-1], axis, up))]
    reduce_scatter x1, waiting for transfers between devices: 272 us -> 0.01 us  [shards(): lax.psum_scatter(qkv_weight_grad.astype(jnp.bfloat16), 'fsdp', scatter_di...]
    unnamed x12, waiting for transfers between devices: 1110 us -> 972 us
  transfers between devices with their start and end apart: 10 -> 13, of which waited for: 8 -> 8; matrix products, arithmetic and copies ran while one was open for 7% -> 7% of each run, Pallas kernels for 0% -> 0%
where the time goes in v1:
time: 7710 us; the launch traced here: 7690 us
  blocking collectives  4110 us (53%)
  waiting for transfers between devices  2840 us (37%)
  matrix products  341 us (4%)
  local copies, waits for them, and re-layouts  241 us (3%)
  other arithmetic  86.8 us (1%)
    psum x1, blocking collectives, shards(): lax.psum((key_grad_all[:, :SUMM], value_grad_all[:, :SUMM]), 'ctx')  2490 us
    psum x1, blocking collectives, shards(): lax.psum((shares[0], shares[1], shares[2], shares[3], shares[4], shares[5...  975 us
    unnamed x12, waiting for transfers between devices  972 us
    all_gather x1, waiting for transfers between devices, shards(): lax.all_gather(up_weight, 'fsdp', axis=0, tiled=True)  553 us
    all_gather x1, waiting for transfers between devices, shards(): lax.all_gather(down_weight, 'fsdp', axis=0, tiled=True)  526 us
    all_gather x1, blocking collectives, shards(): lax.all_gather(down_bias, 'fsdp', axis=0, tiled=True)  495 us
    ppermute x2, waiting for transfers between devices, ring_gather(): earlier.append(lax.ppermute(earlier[-1], axis, up))  364 us
    all_gather x1, waiting for transfers between devices, shards(): lax.all_gather(qkv_weight, 'fsdp', axis=0, tiled=True)  334 us
  transfers between devices with their start and end apart: 13, of which 8 were waited for; matrix products, arithmetic and copies ran while one was open for 7% of the time, Pallas kernels for 0%

profile of v1, /device:TPU:1, one launch (start us, length us, event | category | flops | bytes accessed | tf_op | source)
XLA Modules:
  0.0 7693.5 jit_solution(2250634478453589861)
XLA Ops:
  8.7 10.3 all-gather.2
  19.7 9.3 all-gather.3
  29.7 36.0 all-gather.4
  66.3 33.2 all-gather.5
  103.3 334.1 %all-gather.17.cloned.1.call-done = bf16[2048,6144]{1,0:T(8,128)(2,1)} async-done(((bf16[512,6144]{1,0:T(8,128)(2,1)}), bf16[2048,6144]{1,0:T(8,128)(2,1)}) %all-gather.17.cloned.1.call-update) | async-done | bytes 25165840 | tf_op jit(solution)/shard_map/all_gather | solution.py:92
  437.4 11.9 fusion.99
  459.6 9.7 all-gather.6
  469.3 9.7 all-gather.7
  479.0 9.7 all-gather.8
  488.7 10.2 all_gather.60
  540.9 48.0 while.26
  589.0 88.7 %all-gather.19.cloned.1.call-done = bf16[2048,2048]{1,0:T(8,128)(2,1)} async-done(((bf16[512,2048]{1,0:T(8,128)(2,1)}), bf16[2048,2048]{1,0:T(8,128)(2,1)}) %all-gather.19.cloned.1.call-update) | async-done | bytes 8388624 | tf_op jit(solution)/shard_map/all_gather | solution.py:95
  686.1 552.7 %all-gather.21.cloned.1.call-done = bf16[2048,8192]{1,0:T(8,128)(2,1)} async-done(((bf16[512,8192]{1,0:T(8,128)(2,1)}), bf16[2048,8192]{1,0:T(8,128)(2,1)}) %all-gather.21.cloned.1.call-update) | async-done | bytes 33554448 | tf_op jit(solution)/shard_map/all_gather | solution.py:99
  1238.8 34.7 multiply_convert_fusion.1
  1273.4 526.4 %all-gather.23.cloned.1.call-done = bf16[8192,2048]{1,0:T(8,128)(2,1)} async-done(((bf16[2048,2048]{1,0:T(8,128)(2,1)}), bf16[8192,2048]{1,0:T(8,128)(2,1)}) %all-gather.23.cloned.1.call-update) | async-done | bytes 33554448 | tf_op jit(solution)/shard_map/all_gather | solution.py:192
  1799.8 35.5 fusion.95
  1835.3 17.3 multiply_reduce_fusion.1
  1854.2 8.9 convolution_convert_fusion.3
  1871.6 184.3 %while.27 = (s32[]{:T(128)}, bf16[4,1,272,512]{2,3,1,0:T(8,128)(2,1)}, f32[4,1,1138,512]{2,3,1,0:T(8,128)}, f32[4,1,1138,512]{2,3,1,0:T(8,128)}, s32[4]{0:T(128)...) while((s32[]{:T(128)}, ...), condition=%wide.region_14.15_spmd, body=%wide.region_12.14_spmd.sunk | while | flops 1604632448 | bytes 155238000 | solution.py:253
  1885.9 8.4 multiply_reduce_fusion.8
  1894.3 10.1 multiply_convert_fusion.3
  1932.1 8.4 multiply_reduce_fusion.8
  1940.5 10.1 multiply_convert_fusion.3
  1978.2 8.3 multiply_reduce_fusion.8
  1986.5 10.1 multiply_convert_fusion.3
  2024.2 8.3 multiply_reduce_fusion.8
  2032.5 10.0 multiply_convert_fusion.3
  2055.9 10.1 slice.61
  2073.6 21.4 copy.73
  2095.0 21.4 copy.74
  2117.5 2492.3 %all-reduce.20 = (bf16[1,50,2048]{2,0,1:T(2,128)(2,1)S(1)}, bf16[1,50,2048]{2,0,1:T(2,128)(2,1)S(1)}, bf16[1,1088,2048]{2,0,1:T(2,128)(2,1)}, bf16[1,1088,2048]{2,0,1:T(2,128)(2,1)}) all-reduce(f32[1,50,2048]{2,0,1:T(1,128)S(1)} %copy.76, f32[1,50,2048]{2,0,1:T(1,128)S(1)} %copy.75, ...), channel_id=1, replica_groups=mesh['fsdp'=4,'replica'=2,'ctx'=4] {'ctx'}, use_global_device_ids=true, to_apply=%region_20.21 | all-reduce | flops 4661248 | bytes 27967488 | tf_op jit(solution)/shard_map/psum | solution.py:261
  4626.9 18.3 convolution_convert_fusion.2
  4646.9 24.4 convolution_convert_fusion.1
  4672.5 23.9 convolution_convert_fusion
  4696.5 363.9 %collective-permute-done = bf16[2048,2048]{1,0:T(8,128)(2,1)} collective-permute-done((bf16[2048,2048]{1,0:T(8,128)(2,1)}, bf16[2048,2048]{1,0:T(8,128)(2,1)}, u32[]{:S(2)}, u32[]{:S(2)}) %collective-permute-start) | collective-permute-done | bytes 8388640 | tf_op jit(solution)/shard_map/ppermute | solution.py:22
  5060.3 42.7 collective-permute-start.1
  5106.6 494.9 %all-gather.9 = bf16[4,1,512]{2,1,0:T(2,128)(2,1)S(1)} all-gather(bf16[1,1,512]{2,1,0:T(2,128)(2,1)S(1)} %reshape.399), channel_id=1, replica_groups=mesh['fsdp'=4,'replica'=2,'ctx'=4] {'fsdp'}, dimensions={0}, use_global_device_ids=true | all-gather | bytes 5120 | tf_op jit(solution)/shard_map/all_gather | solution.py:102
  5601.5 8.6 constant_dynamic-update-slice_fusion.11
  5626.6 8.4 constant_dynamic-update-slice_fusion.8
  5635.0 8.3 constant_dynamic-update-slice_fusion.7
  5659.9 8.5 constant_dynamic-update-slice_fusion.4
  5668.4 12.4 fusion.80
  5687.6 14.8 fusion.51
  5702.5 16.6 all-reduce.17
  5724.2 17.7 fusion.40
  5741.9 414.2 %reduce-scatter.13.cloned.1.call-done = bf16[512,8192]{1,0:T(8,128)(2,1)} async-done(((bf16[2048,8192]{1,0:T(8,128)(2,1)}), bf16[512,8192]{1,0:T(8,128)(2,1)}) %reduce-scatter.13.cloned.1.call-update) | async-done | bytes 8388624
  6156.0 555.0 %reduce-scatter.15.cloned.1.call-done = bf16[2048,2048]{1,0:T(8,128)(2,1)} async-done(((bf16[8192,2048]{1,0:T(8,128)(2,1)}), bf16[2048,2048]{1,0:T(8,128)(2,1)}) %reduce-scatter.15.cloned.1.call-update) | async-done | bytes 8388624
  6711.1 975.3 %all-reduce.21 = (f32[512]{0:T(512)}, f32[512]{0:T(512)}, f32[512,6144]{1,0:T(8,128)}, f32[512]{0:T(512)}, f32[512]{0:T(512)}, /*index=5*/f32[512,2048]{1,0:T(8,...) all-reduce(f32[512]{0:T(512)S(1)} %dynamic-slice_convert_fusion.8, ...), channel_id=1, replica_groups=mesh['fsdp'=4,'replica'=2,'ctx'=4] {'replica','ctx'}, use_global_device_ids=true, to_apply=%region_26.27 | all-reduce | flops 12589056 | bytes 75546624 | tf_op jit(solution)/shard_map/psum | solution.py:339
  (352 shorter events, 296.7 us)
Async XLA Ops:
  7.2 95.6 %copy-start.3 = (bf16[1,272,2048]{2,1,0:T(8,128)(2,1)S(1)}, bf16[1,272,2048]{2,1,0:T(8,128)(2,1)}, u32[]{:S(2)}) copy-start(bf16[1,272,2048]{2,1,0:T(8,128)(2,1)} %param.21) | copy-start | bytes 3342340
  7.2 430.2 %all-gather.17.cloned.1.call-start = ((), (), s32[]{:S(2)}) async-start(), calls=%async_computation.4 | async-start | bytes 31457280 | tf_op jit(solution)/shard_map/all_gather | solution.py:92
  7.9 503.1 %all-gather.25.cloned.1.call-start = ((), (), s32[]{:S(2)}) async-start(), calls=%async_computation.10 | async-start | bytes 5570560 | tf_op jit(solution)/shard_map/all_gather | solution.py:144
  19.0 482.4 %copy-start.24 = (f32[4,1,512]{2,1,0:T(1,128)}, f32[4,1,512]{2,1,0:T(1,128)S(1)}, u32[]{:S(2)}) copy-start(f32[4,1,512]{2,1,0:T(1,128)S(1)} %convert_element_type.263) | copy-start | bytes 24580
  101.0 348.3 %copy-start.28 = (f32[272]{0:T(512)}, f32[272]{0:T(512)S(1)}, u32[]{:S(2)}) copy-start(f32[272]{0:T(512)S(1)} %broadcast_multiply_fusion.5) | copy-start | bytes 3268
  102.8 346.5 %copy-start.32 = (f32[272]{0:T(512)}, f32[272]{0:T(512)S(1)}, u32[]{:S(2)}) copy-start(f32[272]{0:T(512)S(1)} %add_rsqrt_fusion.1) | copy-start | bytes 3268
  103.3 346.0 %copy-start.18 = (bf16[272,2048]{1,0:T(8,128)(2,1)}, bf16[272,2048]{1,0:T(8,128)(2,1)S(1)}, u32[]{:S(2)}) copy-start(bf16[272,2048]{1,0:T(8,128)(2,1)S(1)} %fusion.45) | copy-start | bytes 3342340
  454.1 72.7 all-gather.27.cloned.1.call-start
  457.0 220.7 %all-gather.19.cloned.1.call-start = ((), (), s32[]{:S(2)}) async-start(), calls=%async_computation.5 | async-start | bytes 10485760 | tf_op jit(solution)/shard_map/all_gather | solution.py:95
  457.6 11.7 copy-start.48
  457.6 21.4 copy-start.49
  457.6 31.1 copy-start.42
  457.6 41.4 copy-start.52
  457.6 42.6 copy-start.17
  457.6 781.1 %all-gather.21.cloned.1.call-start = ((), (), s32[]{:S(2)}) async-start(), calls=%async_computation.6 | async-start | bytes 41943040 | tf_op jit(solution)/shard_map/all_gather | solution.py:99
  458.2 1341.6 %all-gather.23.cloned.1.call-start = ((), (), s32[]{:S(2)}) async-start(), calls=%async_computation.7 | async-start | bytes 41943040 | tf_op jit(solution)/shard_map/all_gather | solution.py:192
  458.8 5283.1 %reduce-scatter.11.cloned.1.call-start = ((), (), s32[]{:S(2)}) async-start(), calls=%async_computation.9 | async-start | bytes 10485760 | tf_op jit(solution)/shard_map/reduce_scatter | solution.py:320
  479.0 1373.6 %copy-start.26 = (f32[4,1,512]{2,1,0:T(1,128)}, f32[4,1,512]{2,1,0:T(1,128)S(1)}, u32[]{:S(2)}) copy-start(f32[4,1,512]{2,1,0:T(1,128)S(1)} %convert_element_type.268) | copy-start | bytes 24580
  488.7 750.1 %copy-start.38 = (f32[4,1,512]{2,1,0:T(1,128)}, f32[4,1,512]{2,1,0:T(1,128)S(1)}, u32[]{:S(2)}) copy-start(f32[4,1,512]{2,1,0:T(1,128)S(1)} %convert_element_type.269) | copy-start | bytes 24580
  589.0 95.3 %copy-start.1 = (pred[1,1,272,1138]{3,2,1,0:T(8,128)(4,1)}, pred[1,1,272,1138]{3,2,1,0:T(8,128)(4,1)S(1)}, u32[]{:S(2)}) copy-start(pred[1,1,272,1138]{3,2,1,0:T(8,128)(4,1)S(1)} %get-tuple-element.553) | copy-start | bytes 928612
  589.0 95.3 %copy-start.8 = (bf16[1,272,2048]{1,2,0:T(8,128)(2,1)}, bf16[1,272,2048]{1,2,0:T(8,128)(2,1)S(1)}, u32[]{:S(2)}) copy-start(bf16[1,272,2048]{1,2,0:T(8,128)(2,1)S(1)} %get-tuple-element.566) | copy-start | bytes 3342340
  684.3 1168.3 %copy-start.30 = (f32[272]{0:T(512)}, f32[272]{0:T(512)S(1)}, u32[]{:S(2)}) copy-start(f32[272]{0:T(512)S(1)} %broadcast_multiply_fusion.4) | copy-start | bytes 3268
  686.1 1166.6 %copy-start.36 = (f32[272]{0:T(512)}, f32[272]{0:T(512)S(1)}, u32[]{:S(2)}) copy-start(f32[272]{0:T(512)S(1)} %add_rsqrt_fusion) | copy-start | bytes 3268
  1238.8 561.0 %copy-start.13 = (bf16[1,272,2048]{2,1,0:T(8,128)(2,1)S(1)}, bf16[1,272,2048]{2,1,0:T(8,128)(2,1)}, u32[]{:S(2)}) copy-start(bf16[1,272,2048]{2,1,0:T(8,128)(2,1)} %param.24) | copy-start | bytes 3342340
  1799.8 35.5 copy-start.6
  1835.3 17.3 copy-start.53
  1835.3 17.3 copy-start.14
  1863.1 3878.7 %reduce-scatter.9.cloned.1.call-start = ((), (), s32[]{:S(2)}) async-start(), calls=%async_computation.8 | async-start | bytes 31457280 | tf_op jit(solution)/shard_map/reduce_scatter | solution.py:311
  2055.8 11.4 slice-start.2
  2055.9 11.4 slice-start.3
  2055.9 11.4 slice-start.4
  4609.9 11.2 copy-start.11
  4610.0 13.1 copy-start.20
  4610.1 12.9 copy-start.21
  4645.3 1510.8 %reduce-scatter.13.cloned.1.call-start = ((), (), s32[]{:S(2)}) async-start(), calls=%async_computation.12 | async-start | bytes 41943040
  4671.3 2039.8 %reduce-scatter.15.cloned.1.call-start = ((), (), s32[]{:S(2)}) async-start(), calls=%async_computation.13 | async-start | bytes 41943040
  4696.4 408.3 %copy-start.51 = (u32[32]{0:T(128)S(1)}, u32[32]{0:T(128)}, u32[]{:S(2)}) copy-start(u32[32]{0:T(128)} %constant.195) | copy-start | bytes 388
  4696.4 410.2 %copy-start.50 = (bf16[512]{0:T(512)(128)(2,1)S(1)}, bf16[512]{0:T(512)(128)(2,1)}, u32[]{:S(2)}) copy-start(bf16[512]{0:T(512)(128)(2,1)} %param.37) | copy-start | bytes 3076
  4696.4 363.9 %collective-permute-start = (bf16[2048,2048]{1,0:T(8,128)(2,1)}, bf16[2048,2048]{1,0:T(8,128)(2,1)}, u32[]{:S(2)}, u32[]{:S(2)}) collective-permute-start(bf16[2048,2048]{1,0:T(8,128)(2,1)} %param.36), channel_id=1, source_target_pairs={{0,8},{8,16},{16,24},{24,0},{1,9},{9,17},{17,25},{25,1},{2,10},{10... | collective-permute-start | bytes 25165832 | tf_op jit(solution)/shard_map/ppermute | solution.py:22
  5060.3 541.2 %collective-permute-start.1 = (bf16[2048,2048]{1,0:T(8,128)(2,1)}, bf16[2048,2048]{1,0:T(8,128)(2,1)}, u32[]{:S(2)}, u32[]{:S(2)}) collective-permute-start(bf16[2048,2048]{1,0:T(8,128)(2,1)} %collective-permute-done), channel_id=1, source_target_pairs={{0,8},{8,16},{16,24},{24,0},{1,9},{9,17},{17,25},{25,1},{2,10},{10... | collective-permute-start | bytes 25165832 | tf_op jit(solution)/shard_map/ppermute | solution.py:22
  5103.1 523.6 %collective-permute-start.2 = (bf16[2048,2048]{1,0:T(8,128)(2,1)}, bf16[2048,2048]{1,0:T(8,128)(2,1)}, u32[]{:S(2)}, u32[]{:S(2)}) collective-permute-start(bf16[2048,2048]{1,0:T(8,128)(2,1)} %param.36), channel_id=1, source_target_pairs={{0,24},{8,0},{16,8},{24,16},{1,25},{9,1},{17,9},{25,17},{2,26},{10... | collective-permute-start | bytes 25165832 | tf_op jit(solution)/shard_map/ppermute | solution.py:24
  5668.4 19.2 copy-start.4
  5668.4 19.2 copy-start.29
  5668.4 19.2 copy-start.33
  5687.6 14.9 copy-start.34
  5687.6 14.9 copy-start.35
  5687.6 14.9 copy-start.43
  5687.6 14.9 copy-start.44
  (33 other events, 155.7 us)
Sparse Core Ops, SparseCore 0:
  9.6 427.7 all-gather.16
  454.2 34.3 all-gather.24
  490.8 35.9 all-gather.26
  528.2 149.4 all-gather.18
  679.1 559.6 all-gather.20
  1240.2 559.5 all-gather.22
  1863.2 142.2 reduce-scatter.10
  4645.4 844.9 reduce-scatter.8
  5492.9 663.0 reduce-scatter.12
  6158.2 552.7 reduce-scatter.14
